TPU v7x, 128 devices: a whole 4x4x4 slice. The times are simulated.
128 devices in a mesh: seq: 32 (over z, x_lo, y), fsdp: 4 (over x_hi, core).
Axes of the slice: x: 4 (x_hi: 2, x_lo: 2; x = x_hi * 2 + x_lo), y: 4, z: 4, core: 2. Of those that a mesh axis runs over, the one named last changes fastest.
Arguments:
- inputs: bfloat16 [4, 16384, 640], P('fsdp', 'seq'), may hold values from -6 to 6
- doc_start: int32 [4, 16384], P('fsdp', 'seq'), may hold values from 0 to 15360, as said below
- w_query: bfloat16 [640, 1024], P('fsdp'), may hold values from -0.25 to 0.25
- w_key: bfloat16 [640, 256], P('fsdp'), may hold values from -0.25 to 0.25
- w_value: bfloat16 [640, 256], P('fsdp'), may hold values from -0.25 to 0.25
- w_output: bfloat16 [1024, 640], P('fsdp'), may hold values from -0.375 to 0.375
- w_gate: bfloat16 [640, 2048], P('fsdp'), may hold values from -0.25 to 0.25
- w_up: bfloat16 [640, 2048], P('fsdp'), may hold values from -0.25 to 0.25
- w_down: bfloat16 [2048, 640], P('fsdp'), may hold values from -0.125 to 0.125
- norm_attn_in: bfloat16 [640], P('fsdp'), may hold values from 0.099609375 to 1.8984375
- norm_attn_out: bfloat16 [640], P('fsdp'), may hold values from 0.099609375 to 1.8984375
- norm_ffn_in: bfloat16 [640], P('fsdp'), may hold values from 0.099609375 to 1.8984375
- norm_ffn_out: bfloat16 [640], P('fsdp'), may hold values from 0.099609375 to 1.8984375
- norm_query: bfloat16 [256], P('fsdp'), may hold values from 0.099609375 to 1.8984375
- norm_key: bfloat16 [256], P('fsdp'), may hold values from 0.099609375 to 1.8984375
- cotangent: bfloat16 [4, 16384, 640], P('fsdp', 'seq'), may hold values from -6 to 6
Outputs:
- layer_out: bfloat16 [4, 16384, 640], P('fsdp', 'seq')
- input_grad: float32 [4, 16384, 640], P('fsdp', 'seq')
- query_grad: float32 [640, 1024], P('fsdp')
- key_grad: float32 [640, 256], P('fsdp')
- value_grad: float32 [640, 256], P('fsdp')
- output_grad: float32 [1024, 640], P('fsdp')
- gate_grad: float32 [640, 2048], P('fsdp')
- up_grad: float32 [640, 2048], P('fsdp')
- down_grad: float32 [2048, 640], P('fsdp')
- attn_in_grad: float32 [640], P('fsdp')
- attn_out_grad: float32 [640], P('fsdp')
- ffn_in_grad: float32 [640], P('fsdp')
- ffn_out_grad: float32 [640], P('fsdp')
- query_norm_grad: float32 [256], P('fsdp')
- key_norm_grad: float32 [256], P('fsdp')
Inputs may be any that keep to these rules, and one draw needn't show every extreme that they name: Each row of 16384 tokens holds exactly two documents, each of 1024 tokens or more: doc_start is 0 up to the second document's first index and that index from there on; in some row the second document is exactly 1024 tokens long.
All inputs are finite; a program needn't handle non-finite values.
Results may differ from a plain program's by a relative error of at most 0.034.
Values may be sent and summed in bfloat16 or wider, within the bound.
A program may use at most 192 MiB of HBM per device.

v0:
```python
import jax
import jax.numpy as jnp
from jax import lax
from jax.sharding import PartitionSpec as P

WINDOW = 512
epsilon = 1e-06
rope_base = 10000.0
masked_value = -1e30


def side_by_side(arrays, axis, dim, along):
    ends, at = ([], 0)
    for a in arrays[:-1]:
        at += a.shape[along]
        ends.append(at)
    both = jnp.concatenate(arrays, axis=along)
    return tuple(jnp.split(lax.all_gather(both, axis, axis=dim, tiled=True), ends, axis=along))


def from_behind(shard, axis, by):
    count = lax.axis_size(axis)
    pairs = [(i, i + by) for i in range(count) if 0 <= i + by < count]
    return lax.ppermute(shard, axis, pairs)


def side_by_side_2(arrays, axis, dim, along):
    both = jnp.concatenate(arrays, axis=along)
    out, at, gathered = (lax.psum_scatter(both, axis, scatter_dimension=dim, tiled=True), 0, [])
    for a in arrays:
        gathered.append(lax.slice_in_dim(out, at, at + a.shape[along], axis=along))
        at += a.shape[along]
    return tuple(gathered)


def rms_scale(values, gains):
    return values * lax.rsqrt(jnp.mean(values * values, -1, keepdims=True) + epsilon) * gains


def rope_tables(positions, head_width):
    half_width = head_width // 2
    frequency = rope_base ** (-(jnp.arange(half_width, dtype=jnp.float32) * (2.0 / head_width)))
    angles = positions[:, None] * frequency[None, :]
    cosine = jnp.cos(angles)
    sine_part = jnp.sin(angles)
    return (jnp.concatenate([cosine, cosine], -1), jnp.concatenate([sine_part, sine_part], -1))


def rotate(values, cosine, sine_part):
    half_width = values.shape[-1] // 2
    turned = jnp.concatenate([-values[..., half_width:], values[..., :half_width]], -1)
    return values * cosine + turned * sine_part


def forward_dot(left, right):
    return jnp.dot(left, right, preferred_element_type=jnp.float32)


def contract_rows(left, right):
    return lax.dot_general(
        left, right, (((0,), (0,)), ((), ())), preferred_element_type=jnp.float32
    )


def contract_cols(left, right):
    return lax.dot_general(
        left, right, (((1,), (1,)), ((), ())), preferred_element_type=jnp.float32
    )


def gated_product(gate_value, up_value):
    return jax.nn.gelu(gate_value, approximate=True) * up_value


def body(
    inputs,
    doc_start,
    w_query,
    w_key,
    w_value,
    w_output,
    w_gate,
    w_up,
    w_down,
    norm_attn_in,
    norm_attn_out,
    norm_ffn_in,
    norm_ffn_out,
    norm_query,
    norm_key,
    cotangent,
):
    gathered = (
        *side_by_side((w_query, w_key, w_value), "fsdp", 0, 1),
        lax.all_gather(w_output, "fsdp", axis=0, tiled=True),
        *side_by_side((w_gate, w_up), "fsdp", 0, 1),
        lax.all_gather(w_down, "fsdp", axis=0, tiled=True),
        lax.all_gather(norm_attn_in, "fsdp", axis=0, tiled=True),
        lax.all_gather(norm_attn_out, "fsdp", axis=0, tiled=True),
        lax.all_gather(norm_ffn_in, "fsdp", axis=0, tiled=True),
        lax.all_gather(norm_ffn_out, "fsdp", axis=0, tiled=True),
        lax.all_gather(norm_query, "fsdp", axis=0, tiled=True),
        lax.all_gather(norm_key, "fsdp", axis=0, tiled=True),
    )
    full_query, full_key, full_value, full_output, full_gate, full_up, full_down = gathered[:7]
    gain_attn_in, gain_attn_out, gain_ffn_in, gain_ffn_out, gain_query, gain_key = [
        member.astype(jnp.float32) for member in gathered[7:]
    ]
    length = inputs.shape[1]
    head_width = full_key.shape[1]
    head_count = full_query.shape[1] // head_width
    span_count = -(-(WINDOW - 1) // length)
    block_index = lax.axis_index("seq")
    row_index = block_index * length + jnp.arange(length, dtype=jnp.int32)
    doc_local = doc_start[0]
    positions = (row_index - doc_local).astype(jnp.float32)
    cosine, sine_part = rope_tables(positions, head_width)
    source = inputs[0].astype(jnp.float32)
    normed, pull_attn_in = jax.vjp(rms_scale, source, gain_attn_in)
    normed_low = normed.astype(jnp.bfloat16)
    query_raw = forward_dot(normed_low, full_query)
    key_raw = forward_dot(normed_low, full_key)
    value_raw = forward_dot(normed_low, full_value)

    def shape_query(raw_rows, gains):
        return rotate(
            rms_scale(raw_rows.reshape(length, head_count, head_width), gains),
            cosine[:, None, :],
            sine_part[:, None, :],
        )

    def shape_key(raw_rows, gains):
        return rotate(rms_scale(raw_rows, gains), cosine, sine_part)

    query_rows, pull_query = jax.vjp(shape_query, query_raw, gain_query)
    key_rows, pull_key = jax.vjp(shape_key, key_raw, gain_key)
    query_low = query_rows.astype(jnp.bfloat16)
    key_low = key_rows.astype(jnp.bfloat16)
    value_low = value_raw.astype(jnp.bfloat16)
    distance = 1
    key_from, value_from = from_behind((key_low, value_low), "seq", distance)
    earlier_keys = [key_from]
    earlier_values = [value_from]
    all_keys = jnp.concatenate(earlier_keys + [key_low], 0)
    all_values = jnp.concatenate(earlier_values + [value_low], 0)
    key_index = (block_index - span_count) * length + jnp.arange(
        (span_count + 1) * length, dtype=jnp.int32
    )
    visible = (
        (key_index[None, :] >= doc_local[:, None])
        & (key_index[None, :] <= row_index[:, None])
        & (row_index[:, None] - key_index[None, :] < WINDOW)
    )
    score_scale = head_width ** (-0.5)

    def score_rows():
        raw_scores = (
            jnp.einsum("thd,kd->htk", query_low, all_keys, preferred_element_type=jnp.float32)
            * score_scale
        )
        return jnp.where(visible[None], raw_scores, masked_value)

    scores = score_rows()
    row_max = jnp.max(scores, -1, keepdims=True)
    shifted = jnp.exp(scores - row_max)
    row_total = jnp.sum(shifted, -1, keepdims=True)
    soft_weights = shifted / row_total
    log_total = row_max + jnp.log(row_total)
    weights_low = soft_weights.astype(jnp.bfloat16)
    attended = jnp.einsum(
        "htk,kd->thd", weights_low, all_values, preferred_element_type=jnp.float32
    )
    attended = attended.reshape(length, head_count * head_width).astype(jnp.bfloat16)
    projected = forward_dot(attended, full_output)
    branch_one, pull_attn_out = jax.vjp(rms_scale, projected, gain_attn_out)
    hidden_one = source + branch_one
    normed_two, pull_ffn_in = jax.vjp(rms_scale, hidden_one, gain_ffn_in)
    normed_two_low = normed_two.astype(jnp.bfloat16)
    gate_value = forward_dot(normed_two_low, full_gate)
    up_value = forward_dot(normed_two_low, full_up)
    product, pull_product = jax.vjp(gated_product, gate_value, up_value)
    product_low = product.astype(jnp.bfloat16)
    down_value = forward_dot(product_low, full_down)
    branch_two, pull_ffn_out = jax.vjp(rms_scale, down_value, gain_ffn_out)
    layer_out = (hidden_one + branch_two).astype(jnp.bfloat16)[None]
    again = (
        *side_by_side((w_query, w_key, w_value), "fsdp", 0, 1),
        lax.all_gather(w_output, "fsdp", axis=0, tiled=True),
        *side_by_side((w_gate, w_up), "fsdp", 0, 1),
        lax.all_gather(w_down, "fsdp", axis=0, tiled=True),
    )
    back_query, back_key, back_value, back_output, back_gate, back_up, back_down = again
    upstream = cotangent[0].astype(jnp.float32)
    d_down, grad_ffn_out = pull_ffn_out(upstream)
    d_down_low = d_down.astype(jnp.bfloat16)
    grad_down = contract_rows(product_low, d_down_low)
    d_product = contract_cols(d_down_low, back_down)
    d_gate, d_up = pull_product(d_product)
    d_gate_low = d_gate.astype(jnp.bfloat16)
    d_up_low = d_up.astype(jnp.bfloat16)
    grad_gate = contract_rows(normed_two_low, d_gate_low)
    grad_up = contract_rows(normed_two_low, d_up_low)
    d_normed_two = contract_cols(d_gate_low, back_gate) + contract_cols(d_up_low, back_up)
    d_hidden_part, grad_ffn_in = pull_ffn_in(d_normed_two)
    d_hidden = upstream + d_hidden_part
    d_projected, grad_attn_out = pull_attn_out(d_hidden)
    d_projected_low = d_projected.astype(jnp.bfloat16)
    grad_output = contract_rows(attended, d_projected_low)
    d_attended = (
        contract_cols(d_projected_low, back_output)
        .astype(jnp.bfloat16)
        .reshape(length, head_count, head_width)
    )
    soft_again = jnp.exp(score_rows() - log_total)
    d_soft = jnp.einsum("thd,kd->htk", d_attended, all_values, preferred_element_type=jnp.float32)
    inner_sum = jnp.sum(soft_again * d_soft, -1, keepdims=True)
    d_scores = (soft_again * (d_soft - inner_sum)).astype(jnp.bfloat16)
    d_queries = (
        jnp.einsum("htk,kd->thd", d_scores, all_keys, preferred_element_type=jnp.float32)
        * score_scale
    )
    d_keys = (
        jnp.einsum("htk,thd->kd", d_scores, query_low, preferred_element_type=jnp.float32)
        * score_scale
    )
    d_values = jnp.einsum(
        "htk,thd->kd",
        soft_again.astype(jnp.bfloat16),
        d_attended,
        preferred_element_type=jnp.float32,
    )
    d_key_own = d_keys[span_count * length :]
    d_value_own = d_values[span_count * length :]
    distance = 1
    first_row = (span_count - distance) * length
    key_back = from_behind(
        d_keys[first_row : first_row + length].astype(jnp.bfloat16), "seq", -distance
    ).astype(jnp.float32)
    value_back = from_behind(
        d_values[first_row : first_row + length].astype(jnp.bfloat16), "seq", -distance
    ).astype(jnp.float32)
    d_key_own = d_key_own + key_back
    d_value_own = d_value_own + value_back
    d_key_raw, grad_key_norm = pull_key(d_key_own)
    d_query_raw, grad_query_norm = pull_query(d_queries)
    d_query_low = d_query_raw.astype(jnp.bfloat16)
    d_key_low = d_key_raw.astype(jnp.bfloat16)
    d_value_low = d_value_own.astype(jnp.bfloat16)
    grad_query = contract_rows(normed_low, d_query_low)
    grad_key = contract_rows(normed_low, d_key_low)
    grad_value = contract_rows(normed_low, d_value_low)
    d_normed = (
        contract_cols(d_query_low, back_query)
        + contract_cols(d_key_low, back_key)
        + contract_cols(d_value_low, back_value)
    )
    d_source, grad_attn_in = pull_attn_in(d_normed)
    input_grad = (d_hidden + d_source)[None]
    shares = (
        *tuple(
            (
                part.astype(jnp.float32)
                for part in side_by_side_2(
                    (
                        grad_query.astype(jnp.bfloat16),
                        grad_key.astype(jnp.bfloat16),
                        grad_value.astype(jnp.bfloat16),
                    ),
                    "fsdp",
                    0,
                    1,
                )
            )
        ),
        lax.psum_scatter(
            grad_output.astype(jnp.bfloat16), "fsdp", scatter_dimension=0, tiled=True
        ).astype(jnp.float32),
        *tuple(
            (
                part.astype(jnp.float32)
                for part in side_by_side_2(
                    (grad_gate.astype(jnp.bfloat16), grad_up.astype(jnp.bfloat16)), "fsdp", 0, 1
                )
            )
        ),
        lax.psum_scatter(
            grad_down.astype(jnp.bfloat16), "fsdp", scatter_dimension=0, tiled=True
        ).astype(jnp.float32),
        lax.psum_scatter(
            grad_attn_in.astype(jnp.bfloat16), "fsdp", scatter_dimension=0, tiled=True
        ).astype(jnp.float32),
        lax.psum_scatter(
            grad_attn_out.astype(jnp.bfloat16), "fsdp", scatter_dimension=0, tiled=True
        ).astype(jnp.float32),
        lax.psum_scatter(
            grad_ffn_in.astype(jnp.bfloat16), "fsdp", scatter_dimension=0, tiled=True
        ).astype(jnp.float32),
        lax.psum_scatter(
            grad_ffn_out.astype(jnp.bfloat16), "fsdp", scatter_dimension=0, tiled=True
        ).astype(jnp.float32),
        lax.psum_scatter(
            grad_query_norm.astype(jnp.bfloat16), "fsdp", scatter_dimension=0, tiled=True
        ).astype(jnp.float32),
        lax.psum_scatter(
            grad_key_norm.astype(jnp.bfloat16), "fsdp", scatter_dimension=0, tiled=True
        ).astype(jnp.float32),
    )
    finals = (
        lax.psum(shares[0].astype(jnp.bfloat16), "seq").astype(jnp.float32),
        lax.psum(shares[1].astype(jnp.bfloat16), "seq").astype(jnp.float32),
        lax.psum(shares[2].astype(jnp.bfloat16), "seq").astype(jnp.float32),
        lax.psum(shares[3].astype(jnp.bfloat16), "seq").astype(jnp.float32),
        lax.psum(shares[4].astype(jnp.bfloat16), "seq").astype(jnp.float32),
        lax.psum(shares[5].astype(jnp.bfloat16), "seq").astype(jnp.float32),
        lax.psum(shares[6].astype(jnp.bfloat16), "seq").astype(jnp.float32),
        lax.psum(shares[7].astype(jnp.bfloat16), "seq").astype(jnp.float32),
        lax.psum(shares[8].astype(jnp.bfloat16), "seq").astype(jnp.float32),
        lax.psum(shares[9].astype(jnp.bfloat16), "seq").astype(jnp.float32),
        lax.psum(shares[10].astype(jnp.bfloat16), "seq").astype(jnp.float32),
        lax.psum(shares[11].astype(jnp.bfloat16), "seq").astype(jnp.float32),
        lax.psum(shares[12].astype(jnp.bfloat16), "seq").astype(jnp.float32),
    )
    return (
        layer_out,
        input_grad,
        finals[0],
        finals[1],
        finals[2],
        finals[3],
        finals[4],
        finals[5],
        finals[6],
        finals[7],
        finals[8],
        finals[9],
        finals[10],
        finals[11],
        finals[12],
    )


def solution(mesh):
    in_specs = (
        P("fsdp", "seq", None),
        P("fsdp", "seq"),
        P("fsdp", None),
        P("fsdp", None),
        P("fsdp", None),
        P("fsdp", None),
        P("fsdp", None),
        P("fsdp", None),
        P("fsdp", None),
        P("fsdp"),
        P("fsdp"),
        P("fsdp"),
        P("fsdp"),
        P("fsdp"),
        P("fsdp"),
        P("fsdp", "seq", None),
    )
    out_specs = (
        P("fsdp", "seq", None),
        P("fsdp", "seq", None),
        P("fsdp", None),
        P("fsdp", None),
        P("fsdp", None),
        P("fsdp", None),
        P("fsdp", None),
        P("fsdp", None),
        P("fsdp", None),
        P("fsdp"),
        P("fsdp"),
        P("fsdp"),
        P("fsdp"),
        P("fsdp"),
        P("fsdp"),
    )
    return jax.shard_map(body, mesh=mesh, in_specs=in_specs, out_specs=out_specs, check_vma=False)
```

profile of v0, /device:TPU:0, one launch (start us, length us, event | category | flops | bytes accessed | tf_op | source)
XLA Modules:
  0.0 709.7 jit_solution(8686373132811952509)
XLA Ops:
  15.6 10.3 %all-reduce.19 = (bf16[640]{0:T(1024)(128)(2,1)S(1)}, bf16[256]{0:T(256)(128)(2,1)S(1)}, bf16[256]{0:T(256)(128)(2,1)S(1)}, bf16[640]{0:T(1024)(128)(2,1)S(1)}, ...) all-reduce(bf16[640]{0:T(1024)(128)(2,1)S(1)} %dynamic-update-slice, ...), channel_id=1, replica_groups=mesh['seq'=32,'fsdp'=4] {'fsdp'}, use_global_device_ids=true, to_apply=%add.4 | all-reduce | flops 3072 | bytes 12288
  30.2 8.4 %all-gather.5.cloned.1.call-done = bf16[640,1536]{1,0:T(8,128)(2,1)} async-done(((bf16[160,1536]{1,0:T(8,128)(2,1)}), bf16[640,1536]{1,0:T(8,128)(2,1)}) %all-gather.5.cloned.1.call-update) | async-done | bytes 1966096 | tf_op jit(solution)/shard_map/all_gather | solution.py:18
  40.8 4.1 collective-permute-start
  47.6 3.9 collective-permute-start.1
  53.1 2.4 multiply_reduce_fusion.2
  58.5 2.6 fusion.106
  64.5 2.6 fusion.39
  67.1 2.8 multiply_reduce_fusion.9
  72.5 41.2 %all-gather.9.cloned.1.call-done = bf16[640,4096]{1,0:T(8,128)(2,1)} async-done(((bf16[160,4096]{1,0:T(8,128)(2,1)}), bf16[640,4096]{1,0:T(8,128)(2,1)}) %all-gather.9.cloned.1.call-update) | async-done | bytes 5242896 | tf_op jit(solution)/shard_map/all_gather | solution.py:18
  113.6 3.9 fusion.22
  119.5 4.5 multiply_convert_fusion.1
  124.0 20.2 %all-gather.11.cloned.1.call-done = bf16[2048,640]{1,0:T(8,128)(2,1)} async-done(((bf16[512,640]{1,0:T(8,128)(2,1)}), bf16[2048,640]{1,0:T(8,128)(2,1)}) %all-gather.11.cloned.1.call-update) | async-done | bytes 2621456 | tf_op jit(solution)/shard_map/all_gather | solution.py:97
  144.2 4.4 multiply_reduce_fusion.7
  150.6 4.7 fusion.11
  163.2 2.8 fusion
  166.0 2.7 fusion.2
  174.3 7.0 collective-permute-done.2
  190.9 3.3 convolution_convert_fusion.2
  195.8 2.7 pad_maximum_fusion
  199.6 3.3 convolution_convert_fusion.3
  202.9 5.2 convolution_convert_fusion
  208.2 22.5 %reduce-scatter.5.cloned.1.call-done = bf16[160,1536]{1,0:T(8,128)(2,1)} async-done(((bf16[640,1536]{1,0:T(8,128)(2,1)}), bf16[160,1536]{1,0:T(8,128)(2,1)}) %reduce-scatter.5.cloned.1.call-update) | async-done | bytes 491536 | tf_op jit(solution)/shard_map/reduce_scatter | solution.py:29
  234.1 57.1 %reduce-scatter.9.cloned.1.call-done = bf16[160,4096]{1,0:T(8,128)(2,1)} async-done(((bf16[640,4096]{1,0:T(8,128)(2,1)}), bf16[160,4096]{1,0:T(8,128)(2,1)}) %reduce-scatter.9.cloned.1.call-update) | async-done | bytes 1310736 | tf_op jit(solution)/shard_map/reduce_scatter | solution.py:29
  291.2 2.5 fusion.102
  293.7 33.6 %reduce-scatter.7.cloned.1.call-done = bf16[256,640]{1,0:T(8,128)(2,1)} async-done(((bf16[1024,640]{1,0:T(8,128)(2,1)}), bf16[256,640]{1,0:T(8,128)(2,1)}) %reduce-scatter.7.cloned.1.call-update) | async-done | bytes 327696 | tf_op jit(solution)/shard_map/reduce_scatter | solution.py:275
  327.3 43.9 %reduce-scatter.11.cloned.1.call-done = bf16[512,640]{1,0:T(8,128)(2,1)} async-done(((bf16[2048,640]{1,0:T(8,128)(2,1)}), bf16[512,640]{1,0:T(8,128)(2,1)}) %reduce-scatter.11.cloned.1.call-update) | async-done | bytes 655376 | tf_op jit(solution)/shard_map/reduce_scatter | solution.py:286
  372.5 2.2 fusion.59
  376.0 2.7 fusion.49
  378.7 7.4 %all-reduce.18 = (bf16[640]{0:T(1024)(128)(2,1)S(1)}, bf16[640]{0:T(1024)(128)(2,1)S(1)}, bf16[640]{0:T(1024)(128)(2,1)S(1)}, bf16[640]{0:T(1024)(128)(2,1)S(1)}...) all-reduce(bf16[640]{0:T(1024)(128)(2,1)S(1)} %get-tuple-element.23, ...), channel_id=6, replica_groups=mesh['seq'=32,'fsdp'=4] {'fsdp'}, use_global_device_ids=true, to_apply=%region_27.28.clone | all-reduce | flops 3072 | bytes 12288
  386.6 83.4 %all-reduce.16 = (bf16[160]{0:T(256)(128)(2,1)S(1)}, bf16[160]{0:T(256)(128)(2,1)S(1)}, bf16[160]{0:T(256)(128)(2,1)S(1)}, bf16[160]{0:T(256)(128)(2,1)S(1)}, bf...) all-reduce(bf16[160]{0:T(256)(128)(2,1)S(1)} %dynamic-slice.7, ...), channel_id=1, replica_groups=mesh['seq'=32,'fsdp'=4] {'seq'}, use_global_device_ids=true, to_apply=%region_28.29 | all-reduce | flops 768 | bytes 3072 | tf_op jit(solution)/shard_map/psum | solution.py:316
  473.3 2.7 fusion.57
  476.0 216.3 %all-reduce.22.cloned.1.call-done = (bf16[160,1024]{1,0:T(8,128)(2,1)}, bf16[160,256]{1,0:T(8,128)(2,1)}, bf16[160,256]{1,0:T(8,128)(2,1)}, bf16[256,640]{1,0:T(...) async-done(((bf16[160,1024]{1,0:T(8,128)(2,1)}, bf16[160,256]{1,0:T(8,128)(2,1)}, bf16[160,256]{1,0:T(8,128)(2,1)}, ...) | async-done | bytes 2785296 | tf_op jit(solution)/shard_map/psum | solution.py:309
  (280 shorter events, 74.5 us)
Async XLA Ops:
  7.2 31.5 %all-gather.5.cloned.1.call-start = ((), (), s32[]{:S(2)}) async-start(), calls=%async_computation.4 | async-start | bytes 2457600 | tf_op jit(solution)/shard_map/all_gather | solution.py:18
  9.2 57.9 %all-gather.7.cloned.1.call-start = ((), (), s32[]{:S(2)}) async-start(), calls=%async_computation.5 | async-start | bytes 1638400 | tf_op jit(solution)/shard_map/all_gather | solution.py:95
  10.1 103.5 %all-gather.9.cloned.1.call-start = ((), (), s32[]{:S(2)}) async-start(), calls=%async_computation.6 | async-start | bytes 6553600 | tf_op jit(solution)/shard_map/all_gather | solution.py:18
  11.3 132.9 %all-gather.11.cloned.1.call-start = ((), (), s32[]{:S(2)}) async-start(), calls=%async_computation.7 | async-start | bytes 3276800 | tf_op jit(solution)/shard_map/all_gather | solution.py:97
  11.9 218.8 %reduce-scatter.5.cloned.1.call-start = ((), (), s32[]{:S(2)}) async-start(), calls=%async_computation.8 | async-start | bytes 2457600 | tf_op jit(solution)/shard_map/reduce_scatter | solution.py:29
  14.1 32.3 %copy-start.47 = (f32[512]{0:T(512)}, f32[512]{0:T(512)S(1)}, u32[]{:S(2)}) copy-start(f32[512]{0:T(512)S(1)} %fusion.50) | copy-start | bytes 6148
  14.1 38.9 %copy-start.45 = (f32[512]{0:T(512)}, f32[512]{0:T(512)S(1)}, u32[]{:S(2)}) copy-start(f32[512]{0:T(512)S(1)} %fusion.84) | copy-start | bytes 6148
  26.5 20.1 %copy-start.49 = (f32[256]{0:T(256)}, f32[256]{0:T(256)S(1)}, u32[]{:S(2)}) copy-start(f32[256]{0:T(256)S(1)} %convert_element_type.231) | copy-start | bytes 3076
  26.5 26.6 %copy-start.38 = (f32[640]{0:T(1024)}, f32[640]{0:T(1024)S(1)}, u32[]{:S(2)}) copy-start(f32[640]{0:T(1024)S(1)} %convert_element_type.228) | copy-start | bytes 7684
  30.2 16.4 %copy-start.11 = (f32[512,128]{0,1:T(8,128)}, f32[512,128]{0,1:T(8,128)S(1)}, u32[]{:S(2)}) copy-start(f32[512,128]{0,1:T(8,128)S(1)} %get-tuple-element.79) | copy-start | bytes 786436
  30.2 16.4 %copy-start.13 = (f32[512,128]{0,1:T(8,128)}, f32[512,128]{0,1:T(8,128)S(1)}, u32[]{:S(2)}) copy-start(f32[512,128]{0,1:T(8,128)S(1)} %get-tuple-element.80) | copy-start | bytes 786436
  40.8 21.6 %collective-permute-start = (bf16[512,256]{1,0:T(8,128)(2,1)}, bf16[512,256]{1,0:T(8,128)(2,1)}, u32[]{:S(2)}, u32[]{:S(2)}) collective-permute-start(bf16[512,256]{1,0:T(8,128)(2,1)} %convolution_convert_fusion.8), channel_id=1, source_target_pairs={{0,4},{4,8},{8,12},{12,16},{16,20},{20,24},{24,28},{28,32},{32,36}... | collective-permute-start | bytes 786440 | tf_op jit(solution)/shard_map/ppermute | solution.py:24
  47.6 10.7 %copy-start.18 = (bf16[512,256]{0,1:T(8,128)(2,1)}, bf16[512,256]{0,1:T(8,128)(2,1)S(1)}, u32[]{:S(2)}) copy-start(bf16[512,256]{0,1:T(8,128)(2,1)S(1)} %get-tuple-element.76) | copy-start | bytes 786436
  47.6 10.6 %collective-permute-start.1 = (bf16[512,256]{0,1:T(8,128)(2,1)S(1)}, bf16[512,256]{0,1:T(8,128)(2,1)}, u32[]{:S(2)}, u32[]{:S(2)}) collective-permute-start(bf16[512,256]{0,1:T(8,128)(2,1)S(1)} %get-tuple-element.76), channel_id=1, source_target_pairs={{0,4},{4,8},{8,12},{12,16},{16,20},{20,24},{24,28},{28,32},{32,36}... | collective-permute-start | bytes 786440 | tf_op jit(solution)/shard_map/ppermute | solution.py:24
  144.2 6.4 copy-start.68
  144.2 6.4 copy-start.72
  149.2 6.1 slice-start.2
  155.3 7.9 %slice-start = ((s8[8388608]{0:T(1024)(128)(4,1)}), s8[4194304]{0:T(1024)(128)(4,1)S(1)}, s32[]{:S(2)}) async-start(s8[8388608]{0:T(1024)(128)(4,1)} %bitcast.145), calls=%async_computation.13 | async-start | bytes 8388608
  170.1 11.2 %copy-start.14 = (f32[512,128]{0,1:T(8,128)S(1)}, f32[512,128]{0,1:T(8,128)}, u32[]{:S(2)}) copy-start(f32[512,128]{0,1:T(8,128)} %copy-done.13) | copy-start | bytes 786436
  170.1 11.2 %collective-permute-start.2 = (bf16[512,256]{0,1:T(8,128)(2,1)S(1)}, bf16[512,256]{0,1:T(8,128)(2,1)S(1)}, u32[]{:S(2)}, u32[]{:S(2)}) collective-permute-start(bf16[512,256]{0,1:T(8,128)(2,1)S(1)} %slice.82), channel_id=1, source_target_pairs={{4,0},{8,4},{12,8},{16,12},{20,16},{24,20},{28,24},{32,28},{36,32}... | collective-permute-start | bytes 786440 | tf_op jit(solution)/shard_map/ppermute | solution.py:24
  172.8 16.0 %copy-start.34 = (f32[1024,256]{1,0:T(8,128)}, f32[1024,256]{1,0:T(8,128)S(1)}, u32[]{:S(2)}) copy-start(f32[1024,256]{1,0:T(8,128)S(1)} %fusion.40) | copy-start | bytes 3145732
  172.8 8.6 %copy-start.19 = (bf16[512,256]{0,1:T(8,128)(2,1)S(1)}, bf16[512,256]{0,1:T(8,128)(2,1)}, u32[]{:S(2)}) copy-start(bf16[512,256]{0,1:T(8,128)(2,1)} %copy-done.18) | copy-start | bytes 786436
  172.8 16.0 %collective-permute-start.3 = (bf16[512,256]{1,0:T(8,128)(2,1)S(1)}, bf16[512,256]{1,0:T(8,128)(2,1)S(1)}, u32[]{:S(2)}, u32[]{:S(2)}) collective-permute-start(bf16[512,256]{1,0:T(8,128)(2,1)S(1)} %slice.81), channel_id=1, source_target_pairs={{4,0},{8,4},{12,8},{16,12},{20,16},{24,20},{28,24},{32,28},{36,32}... | collective-permute-start | bytes 786440 | tf_op jit(solution)/shard_map/ppermute | solution.py:24
  190.9 100.3 %reduce-scatter.9.cloned.1.call-start = ((), (), s32[]{:S(2)}) async-start(), calls=%async_computation.10 | async-start | bytes 6553600 | tf_op jit(solution)/shard_map/reduce_scatter | solution.py:29
  198.5 128.7 %reduce-scatter.7.cloned.1.call-start = ((), (), s32[]{:S(2)}) async-start(), calls=%async_computation.9 | async-start | bytes 1638400 | tf_op jit(solution)/shard_map/reduce_scatter | solution.py:275
  202.9 168.3 %reduce-scatter.11.cloned.1.call-start = ((), (), s32[]{:S(2)}) async-start(), calls=%async_computation.11 | async-start | bytes 3276800 | tf_op jit(solution)/shard_map/reduce_scatter | solution.py:286
  208.2 484.2 %all-reduce.22.cloned.1.call-start = ((), (), s32[]{:S(2)}) async-start(), calls=%async_computation.12 | async-start | bytes 5570560 | tf_op jit(solution)/shard_map/psum | solution.py:309
  234.1 138.5 %copy-start.17 = (bf16[640,1536]{1,0:T(8,128)(2,1)S(1)}, bf16[640,1536]{1,0:T(8,128)(2,1)}, u32[]{:S(2)}) copy-start(bf16[640,1536]{1,0:T(8,128)(2,1)} %all-gather.5.cloned.1.call-done) | copy-start | bytes 5898244
  376.0 97.3 %copy-start.48 = (f32[512]{0:T(512)S(1)}, f32[512]{0:T(512)}, u32[]{:S(2)}) copy-start(f32[512]{0:T(512)} %copy-done.47) | copy-start | bytes 6148
  376.0 97.3 %copy-start.4 = (f32[512,640]{1,0:T(8,128)S(1)}, f32[512,640]{1,0:T(8,128)}, u32[]{:S(2)}) copy-start(f32[512,640]{1,0:T(8,128)} %copy-done.3) | copy-start | bytes 3932164
  692.4 7.0 copy-start.33
  694.0 6.6 copy-start.32
  (58 other events, 157.4 us)
Sparse Core Ops, SparseCore 0:
  10.3 28.3 all-gather.4
  40.3 21.7 all-gather.6
  64.4 49.1 all-gather.8
  115.1 29.0 all-gather.10
  191.0 39.6 reduce-scatter.4
  233.4 57.7 reduce-scatter.8
  294.4 32.8 reduce-scatter.6
  330.1 41.0 reduce-scatter.10
  374.8 317.4 all-reduce.21
where the time goes:
time: 715 us; the launch traced here: 710 us
  waiting for transfers between devices  452 us (63%)
  blocking collectives  101 us (14%)
  matrix products  64.8 us (9%)
  other arithmetic  41.5 us (6%)
  local copies, waits for them, and re-layouts  21.3 us (3%)
  between operations  17.9 us (3%)
  starting transfers between devices  11.4 us (2%)
    psum x1, waiting for transfers between devices, body(): lax.psum(shares[0].astype(jnp.bfloat16), 'seq').astype(jnp.float32)  216 us
    psum x1, blocking collectives, body(): lax.psum(shares[7].astype(jnp.bfloat16), 'seq').astype(jnp.float32)  83.4 us
    reduce_scatter x2, waiting for transfers between devices, side_by_side_2(): lax.psum_scatter(both, axis, scatter_dimension=dim, tiled=True)  79.6 us
    all_gather x2, waiting for transfers between devices, side_by_side(): lax.all_gather(both, axis, axis=dim, tiled=True)  49.6 us
    reduce_scatter x1, waiting for transfers between devices, body(): lax.psum_scatter(grad_down.astype(jnp.bfloat16), 'fsdp', scatter_dimensio...  43.9 us
    reduce_scatter x1, waiting for transfers between devices, body(): lax.psum_scatter(grad_output.astype(jnp.bfloat16), 'fsdp', scatter_dimens...  33.6 us
    dot_general x7, matrix products, forward_dot(): return jnp.dot(left, right, preferred_element_type=jnp.float32)  21.6 us
    all_gather x1, waiting for transfers between devices, body(): lax.all_gather(w_down, 'fsdp', axis=0, tiled=True)  20.2 us
  transfers between devices with their start and end apart: 13, of which 9 were waited for; matrix products, arithmetic and copies ran while one was open for 11% of the time, Pallas kernels for 0%

commit v1 on v0

--- a/solution.py
+++ b/solution.py
@@ -2,6 +2,7 @@
 import jax.numpy as jnp
 from jax import lax
 from jax.sharding import PartitionSpec as P
+from jax.lax import all_gather
 
 WINDOW = 512
 epsilon = 1e-06
@@ -306,7 +307,7 @@
         ).astype(jnp.float32),
     )
     finals = (
-        lax.psum(shares[0].astype(jnp.bfloat16), "seq").astype(jnp.float32),
+        jnp.sum(all_gather(shares[0].astype(jnp.bfloat16), "seq"), axis=0).astype(jnp.float32),
         lax.psum(shares[1].astype(jnp.bfloat16), "seq").astype(jnp.float32),
         lax.psum(shares[2].astype(jnp.bfloat16), "seq").astype(jnp.float32),
         lax.psum(shares[3].astype(jnp.bfloat16), "seq").astype(jnp.float32),

time: 715 us -> 879 us (1.23)
  waiting for transfers between devices: 452 us -> 608 us
    all_gather x0 -> x1, waiting for transfers between devices: none -> 161 us  [body(): all_gather(shares[0].astype(jnp.bfloat16), 'seq')]
  transfers between devices with their start and end apart: 13 -> 14, of which waited for: 9 -> 10; matrix products, arithmetic and copies ran while one was open for 11% -> 10% of each run, Pallas kernels for 0% -> 0%
where the time goes in v1:
time: 879 us; the launch traced here: 874 us
  waiting for transfers between devices  608 us (69%)
  blocking collectives  101 us (11%)
  matrix products  65.5 us (7%)
  other arithmetic  49 us (6%)
  local copies, waits for them, and re-layouts  20.6 us (2%)
  between operations  18.2 us (2%)
  starting transfers between devices  11 us (1%)
    psum x1, waiting for transfers between devices, body(): lax.psum(shares[1].astype(jnp.bfloat16), 'seq').astype(jnp.float32)  210 us
    all_gather x1, waiting for transfers between devices, body(): all_gather(shares[0].astype(jnp.bfloat16), 'seq')  161 us
    psum x1, blocking collectives, body(): lax.psum(shares[7].astype(jnp.bfloat16), 'seq').astype(jnp.float32)  83.4 us
    reduce_scatter x2, waiting for transfers between devices, side_by_side_2(): lax.psum_scatter(both, axis, scatter_dimension=dim, tiled=True)  81.4 us
    all_gather x2, waiting for transfers between devices, side_by_side(): lax.all_gather(both, axis, axis=dim, tiled=True)  50 us
    reduce_scatter x1, waiting for transfers between devices, body(): lax.psum_scatter(grad_down.astype(jnp.bfloat16), 'fsdp', scatter_dimensio...  43.9 us
    reduce_scatter x1, waiting for transfers between devices, body(): lax.psum_scatter(grad_output.astype(jnp.bfloat16), 'fsdp', scatter_dimens...  33.6 us
    dot_general x7, matrix products, forward_dot(): return jnp.dot(left, right, preferred_element_type=jnp.float32)  21.6 us
  transfers between devices with their start and end apart: 14, of which 10 were waited for; matrix products, arithmetic and copies ran while one was open for 10% of the time, Pallas kernels for 0%

profile of v1, /device:TPU:0, one launch (start us, length us, event | category | flops | bytes accessed | tf_op | source)
XLA Modules:
  0.0 873.8 jit_solution(8255931573292414710)
XLA Ops:
  15.6 10.3 %all-reduce.19 = (bf16[640]{0:T(1024)(128)(2,1)S(1)}, bf16[256]{0:T(256)(128)(2,1)S(1)}, bf16[256]{0:T(256)(128)(2,1)S(1)}, bf16[640]{0:T(1024)(128)(2,1)S(1)}, ...) all-reduce(bf16[640]{0:T(1024)(128)(2,1)S(1)} %dynamic-update-slice, ...), channel_id=1, replica_groups=mesh['seq'=32,'fsdp'=4] {'fsdp'}, use_global_device_ids=true, to_apply=%add.4 | all-reduce | flops 3072 | bytes 12288
  30.2 8.4 all-gather.7.cloned.1.call-done
  40.8 4.1 collective-permute-start
  47.6 3.5 collective-permute-start.1
  58.1 2.6 fusion.106
  64.1 2.6 fusion.39
  66.7 2.8 multiply_reduce_fusion.9
  72.1 41.5 %all-gather.11.cloned.1.call-done = bf16[640,4096]{1,0:T(8,128)(2,1)} async-done(((bf16[160,4096]{1,0:T(8,128)(2,1)}), bf16[640,4096]{1,0:T(8,128)(2,1)}) %all-gather.11.cloned.1.call-update) | async-done | bytes 5242896 | tf_op jit(solution)/shard_map/all_gather | solution.py:19
  113.6 3.9 fusion.22
  119.5 4.5 multiply_convert_fusion.1
  124.0 20.2 %all-gather.13.cloned.1.call-done = bf16[2048,640]{1,0:T(8,128)(2,1)} async-done(((bf16[512,640]{1,0:T(8,128)(2,1)}), bf16[2048,640]{1,0:T(8,128)(2,1)}) %all-gather.13.cloned.1.call-update) | async-done | bytes 2621456 | tf_op jit(solution)/shard_map/all_gather | solution.py:98
  144.2 4.4 multiply_reduce_fusion.7
  150.6 4.7 fusion.11
  157.4 2.6 multiply_reduce_fusion.3
  163.8 2.8 fusion
  166.6 2.9 fusion.2
  175.0 7.0 collective-permute-done.2
  192.4 3.3 convolution_convert_fusion.2
  197.3 2.7 pad_maximum_fusion
  201.1 3.3 convolution_convert_fusion.3
  204.5 5.2 convolution_convert_fusion
  209.7 22.5 %reduce-scatter.5.cloned.1.call-done = bf16[160,1536]{1,0:T(8,128)(2,1)} async-done(((bf16[640,1536]{1,0:T(8,128)(2,1)}), bf16[160,1536]{1,0:T(8,128)(2,1)}) %reduce-scatter.5.cloned.1.call-update) | async-done | bytes 491536 | tf_op jit(solution)/shard_map/reduce_scatter | solution.py:30
  233.8 58.8 %reduce-scatter.9.cloned.1.call-done = bf16[160,4096]{1,0:T(8,128)(2,1)} async-done(((bf16[640,4096]{1,0:T(8,128)(2,1)}), bf16[160,4096]{1,0:T(8,128)(2,1)}) %reduce-scatter.9.cloned.1.call-update) | async-done | bytes 1310736 | tf_op jit(solution)/shard_map/reduce_scatter | solution.py:30
  295.2 33.6 %reduce-scatter.7.cloned.1.call-done = bf16[256,640]{1,0:T(8,128)(2,1)} async-done(((bf16[1024,640]{1,0:T(8,128)(2,1)}), bf16[256,640]{1,0:T(8,128)(2,1)}) %reduce-scatter.7.cloned.1.call-update) | async-done | bytes 327696 | tf_op jit(solution)/shard_map/reduce_scatter | solution.py:276
  328.8 43.9 %reduce-scatter.11.cloned.1.call-done = bf16[512,640]{1,0:T(8,128)(2,1)} async-done(((bf16[2048,640]{1,0:T(8,128)(2,1)}), bf16[512,640]{1,0:T(8,128)(2,1)}) %reduce-scatter.11.cloned.1.call-update) | async-done | bytes 655376 | tf_op jit(solution)/shard_map/reduce_scatter | solution.py:287
  378.4 2.7 fusion.49
  381.1 7.5 all-reduce.18
  389.0 83.4 %all-reduce.16 = (bf16[160]{0:T(256)(128)(2,1)S(1)}, bf16[160]{0:T(256)(128)(2,1)S(1)}, bf16[160]{0:T(256)(128)(2,1)S(1)}, bf16[160]{0:T(256)(128)(2,1)S(1)}, bf...) all-reduce(bf16[160]{0:T(256)(128)(2,1)S(1)} %dynamic-slice.7, ...), channel_id=1, replica_groups=mesh['seq'=32,'fsdp'=4] {'seq'}, use_global_device_ids=true, to_apply=%region_28.29 | all-reduce | flops 768 | bytes 3072 | tf_op jit(solution)/shard_map/psum | solution.py:317
  475.7 2.7 fusion.57
  478.5 210.0 %all-reduce.22.cloned.1.call-done = (bf16[160,256]{1,0:T(8,128)(2,1)}, bf16[160,256]{1,0:T(8,128)(2,1)}, bf16[256,640]{1,0:T(8,128)(2,1)}, bf16[160,2048]{1,0:T(...) async-done(((bf16[160,256]{1,0:T(8,128)(2,1)}, bf16[160,256]{1,0:T(8,128)(2,1)}, bf16[256,640]{1,0:T(8,128)(2,1)}, bf16[160,2048]{1,0:T(8,128)(2,1)}, ...) | async-done | bytes 2457616 | tf_op jit(solution)/shard_map/psum | solution.py:311
  698.2 160.9 %all-gather.15.cloned.1.call-done = bf16[5120,1024]{1,0:T(8,128)(2,1)} async-done(((bf16[160,1024]{1,0:T(8,128)(2,1)}), bf16[5120,1024]{1,0:T(8,128)(2,1)}) %all-gather.15.cloned.1.call-update) | async-done | bytes 10485776 | tf_op jit(solution)/shard_map/all_gather | solution.py:310
  859.1 6.7 reduce_sum.212
  (292 shorter events, 79.6 us)
Async XLA Ops:
  7.2 31.5 %all-gather.7.cloned.1.call-start = ((), (), s32[]{:S(2)}) async-start(), calls=%async_computation.4 | async-start | bytes 2457600 | tf_op jit(solution)/shard_map/all_gather | solution.py:19
  9.2 57.5 %all-gather.9.cloned.1.call-start = ((), (), s32[]{:S(2)}) async-start(), calls=%async_computation.5 | async-start | bytes 1638400 | tf_op jit(solution)/shard_map/all_gather | solution.py:96
  10.1 103.5 %all-gather.11.cloned.1.call-start = ((), (), s32[]{:S(2)}) async-start(), calls=%async_computation.6 | async-start | bytes 6553600 | tf_op jit(solution)/shard_map/all_gather | solution.py:19
  11.3 132.9 %all-gather.13.cloned.1.call-start = ((), (), s32[]{:S(2)}) async-start(), calls=%async_computation.7 | async-start | bytes 3276800 | tf_op jit(solution)/shard_map/all_gather | solution.py:98
  11.9 220.3 %reduce-scatter.5.cloned.1.call-start = ((), (), s32[]{:S(2)}) async-start(), calls=%async_computation.8 | async-start | bytes 2457600 | tf_op jit(solution)/shard_map/reduce_scatter | solution.py:30
  14.1 32.2 %copy-start.49 = (f32[512]{0:T(512)}, f32[512]{0:T(512)S(1)}, u32[]{:S(2)}) copy-start(f32[512]{0:T(512)S(1)} %fusion.50) | copy-start | bytes 6148
  14.1 38.6 %copy-start.47 = (f32[512]{0:T(512)}, f32[512]{0:T(512)S(1)}, u32[]{:S(2)}) copy-start(f32[512]{0:T(512)S(1)} %fusion.84) | copy-start | bytes 6148
  26.5 20.0 %copy-start.51 = (f32[256]{0:T(256)}, f32[256]{0:T(256)S(1)}, u32[]{:S(2)}) copy-start(f32[256]{0:T(256)S(1)} %convert_element_type.233) | copy-start | bytes 3076
  26.5 26.2 %copy-start.40 = (f32[640]{0:T(1024)}, f32[640]{0:T(1024)S(1)}, u32[]{:S(2)}) copy-start(f32[640]{0:T(1024)S(1)} %convert_element_type.230) | copy-start | bytes 7684
  30.2 16.4 %copy-start.11 = (f32[512,128]{0,1:T(8,128)}, f32[512,128]{0,1:T(8,128)S(1)}, u32[]{:S(2)}) copy-start(f32[512,128]{0,1:T(8,128)S(1)} %get-tuple-element.78) | copy-start | bytes 786436
  30.2 16.4 %copy-start.13 = (f32[512,128]{0,1:T(8,128)}, f32[512,128]{0,1:T(8,128)S(1)}, u32[]{:S(2)}) copy-start(f32[512,128]{0,1:T(8,128)S(1)} %get-tuple-element.79) | copy-start | bytes 786436
  40.8 21.2 %collective-permute-start = (bf16[512,256]{1,0:T(8,128)(2,1)}, bf16[512,256]{1,0:T(8,128)(2,1)}, u32[]{:S(2)}, u32[]{:S(2)}) collective-permute-start(bf16[512,256]{1,0:T(8,128)(2,1)} %convolution_convert_fusion.8), channel_id=1, source_target_pairs={{0,4},{4,8},{8,12},{12,16},{16,20},{20,24},{24,28},{28,32},{32,36}... | collective-permute-start | bytes 786440 | tf_op jit(solution)/shard_map/ppermute | solution.py:25
  47.6 10.3 %copy-start.18 = (bf16[512,256]{0,1:T(8,128)(2,1)}, bf16[512,256]{0,1:T(8,128)(2,1)S(1)}, u32[]{:S(2)}) copy-start(bf16[512,256]{0,1:T(8,128)(2,1)S(1)} %get-tuple-element.75) | copy-start | bytes 786436
  47.6 10.3 %collective-permute-start.1 = (bf16[512,256]{0,1:T(8,128)(2,1)S(1)}, bf16[512,256]{0,1:T(8,128)(2,1)}, u32[]{:S(2)}, u32[]{:S(2)}) collective-permute-start(bf16[512,256]{0,1:T(8,128)(2,1)S(1)} %get-tuple-element.75), channel_id=1, source_target_pairs={{0,4},{4,8},{8,12},{12,16},{16,20},{20,24},{24,28},{28,32},{32,36}... | collective-permute-start | bytes 786440 | tf_op jit(solution)/shard_map/ppermute | solution.py:25
  144.2 6.4 copy-start.72
  144.2 6.4 copy-start.76
  155.3 8.4 slice-start
  170.8 11.2 %copy-start.14 = (f32[512,128]{0,1:T(8,128)S(1)}, f32[512,128]{0,1:T(8,128)}, u32[]{:S(2)}) copy-start(f32[512,128]{0,1:T(8,128)} %copy-done.13) | copy-start | bytes 786436
  170.8 11.2 %collective-permute-start.2 = (bf16[512,256]{0,1:T(8,128)(2,1)S(1)}, bf16[512,256]{0,1:T(8,128)(2,1)S(1)}, u32[]{:S(2)}, u32[]{:S(2)}) collective-permute-start(bf16[512,256]{0,1:T(8,128)(2,1)S(1)} %slice.82), channel_id=1, source_target_pairs={{4,0},{8,4},{12,8},{16,12},{20,16},{24,20},{28,24},{32,28},{36,32}... | collective-permute-start | bytes 786440 | tf_op jit(solution)/shard_map/ppermute | solution.py:25
  173.5 16.6 %copy-start.33 = (f32[1024,256]{1,0:T(8,128)}, f32[1024,256]{1,0:T(8,128)S(1)}, u32[]{:S(2)}) copy-start(f32[1024,256]{1,0:T(8,128)S(1)} %fusion.40) | copy-start | bytes 3145732
  173.5 8.6 copy-start.19
  173.6 16.6 %collective-permute-start.3 = (bf16[512,256]{1,0:T(8,128)(2,1)S(1)}, bf16[512,256]{1,0:T(8,128)(2,1)S(1)}, u32[]{:S(2)}, u32[]{:S(2)}) collective-permute-start(bf16[512,256]{1,0:T(8,128)(2,1)S(1)} %slice.81), channel_id=1, source_target_pairs={{4,0},{8,4},{12,8},{16,12},{20,16},{24,20},{28,24},{32,28},{36,32}... | collective-permute-start | bytes 786440 | tf_op jit(solution)/shard_map/ppermute | solution.py:25
  192.4 100.3 %reduce-scatter.9.cloned.1.call-start = ((), (), s32[]{:S(2)}) async-start(), calls=%async_computation.10 | async-start | bytes 6553600 | tf_op jit(solution)/shard_map/reduce_scatter | solution.py:30
  200.1 128.7 %reduce-scatter.7.cloned.1.call-start = ((), (), s32[]{:S(2)}) async-start(), calls=%async_computation.9 | async-start | bytes 1638400 | tf_op jit(solution)/shard_map/reduce_scatter | solution.py:276
  204.4 168.3 %reduce-scatter.11.cloned.1.call-start = ((), (), s32[]{:S(2)}) async-start(), calls=%async_computation.11 | async-start | bytes 3276800 | tf_op jit(solution)/shard_map/reduce_scatter | solution.py:287
  209.7 478.8 %all-reduce.22.cloned.1.call-start = ((), (), s32[]{:S(2)}) async-start(), calls=%async_computation.13 | async-start | bytes 4915200 | tf_op jit(solution)/shard_map/psum | solution.py:311
  233.8 138.9 %copy-start.36 = (bf16[160,1536]{1,0:T(8,128)(2,1)S(1)}, bf16[160,1536]{1,0:T(8,128)(2,1)}, u32[]{:S(2)}) copy-start(bf16[160,1536]{1,0:T(8,128)(2,1)} %reduce-scatter.5.cloned.1.call-done) | copy-start | bytes 1474564
  295.2 79.7 %copy-start.17 = (bf16[640,1536]{1,0:T(8,128)(2,1)S(1)}, bf16[640,1536]{1,0:T(8,128)(2,1)}, u32[]{:S(2)}) copy-start(bf16[640,1536]{1,0:T(8,128)(2,1)} %all-gather.7.cloned.1.call-done) | copy-start | bytes 5898244
  372.7 486.4 %all-gather.15.cloned.1.call-start = ((), (), s32[]{:S(2)}) async-start(), calls=%async_computation.12 | async-start | bytes 10813440 | tf_op jit(solution)/shard_map/all_gather | solution.py:310
  378.4 97.3 %copy-start.50 = (f32[512]{0:T(512)S(1)}, f32[512]{0:T(512)}, u32[]{:S(2)}) copy-start(f32[512]{0:T(512)} %copy-done.49) | copy-start | bytes 6148
  378.4 97.3 %copy-start.4 = (f32[512,640]{1,0:T(8,128)S(1)}, f32[512,640]{1,0:T(8,128)}, u32[]{:S(2)}) copy-start(f32[512,640]{1,0:T(8,128)} %copy-done.3) | copy-start | bytes 3932164
  688.5 7.4 copy-start.32
  (63 other events, 174.1 us)
Sparse Core Ops, SparseCore 0:
  10.3 28.3 all-gather.6
  40.3 21.7 all-gather.8
  64.4 49.1 all-gather.10
  115.1 29.0 all-gather.12
  192.5 39.7 reduce-scatter.4
  234.9 57.7 reduce-scatter.8
  295.9 32.8 reduce-scatter.6
  331.6 41.0 reduce-scatter.10
  376.3 312.1 all-reduce.21
  690.0 169.0 all-gather.14
